TPU v7x, 32 devices: a whole 2x2x4 slice. The times are simulated.
32 devices in a mesh: groups: 2 (over x), span: 8 (over z, y), head: 2 (over core).
Axes of the slice: x: 2, y: 2, z: 4, core: 2. Of those that a mesh axis runs over, the one named last changes fastest.
Arguments:
- span_states: bfloat16 [2048, 4096], P(('groups', 'span'), 'head'), parts along dimension 0, may hold values from -1.5 to 1.5
- span_queries: bfloat16 [2048, 2048], P(('groups', 'span'), 'head'), parts along dimension 0, may hold values from -1000 to 1000
- span_memory: bfloat16 [2048, 2, 896], P(('groups', 'span'), None, 'head'), parts along dimension 0, may hold values from -1000 to 1000
- passages: bfloat16 [16384, 896], P(('groups', 'span')), parts along dimension 0, may hold values from -1.5 to 1.5
- neighbours: int32 [32, 2], P(('groups', 'span')), parts along dimension 0, may hold values from 0 to 63, as said below
- enc_query_w: bfloat16 [896, 896], P(None, 'head'), may hold values from -0.1875 to 0.1875
- enc_out_w: bfloat16 [896, 896], P(None, 'head'), may hold values from -0.1875 to 0.1875
- kv_weight: bfloat16 [896, 2, 2048], P(None, None, ('head', 'span')), may hold values from -0.1875 to 0.1875
- out_weight: bfloat16 [2048, 4096], P('head', 'span'), may hold values from -0.125 to 0.125
Outputs:
- mixed_states: bfloat16 [2048, 4096], P(('groups', 'span'), 'head'), parts along dimension 0
There are 2 independent parts, one for each index of `groups`. A program takes and returns all parts, laid end to end along the dimension named above; an argument that names none is the same for every part. Nothing has to cross between parts.
Inputs may be any that keep to these rules, and one draw needn't show every extreme that they name: `neighbours`: passage p belongs to index p // 8 of the span axis. Among the spans of one index of the span axis, all 4 passages listed belong to distinct indices.
All inputs are finite; a program needn't handle non-finite values.
Results may differ from a plain program's by a relative error of at most 0.025.
Values may be sent and summed in bfloat16 or wider, within the bound.
A program may use at most 64 MiB of HBM per device.

v0:
```python
import math
import jax
import jax.numpy as jnp
from jax import lax
from jax.sharding import PartitionSpec as P

HD = 128
E = 896
EHD = 64
CT = 64
PT = 128
NB = 2
PS_DEV = 8
epsilon = 1e-06


def rms_rows(values):
    return values * lax.rsqrt(jnp.mean(values * values, axis=-1, keepdims=True) + epsilon)


def softmax_rows(scores):
    top_score = jnp.max(scores, axis=-1, keepdims=True)
    raised = jnp.exp(scores - top_score)
    return raised / jnp.sum(raised, axis=-1, keepdims=True)


def wanted_slots(owner_flat, local_flat, device_count):
    matched = owner_flat[:, None] == jnp.arange(device_count, dtype=jnp.int32)[None, :]
    return jnp.sum(jnp.where(matched, local_flat[:, None], 0), axis=0)


def fetch_passages(wanted, passages):
    blocks = passages.reshape(-1, PT, E)
    picked = blocks[lax.all_to_all(wanted, "span", split_axis=0, concat_axis=0, tiled=True)]
    return lax.all_to_all(picked, "span", split_axis=0, concat_axis=0, tiled=True)


def encode_branch(copies, memory, query_w, out_w):
    groups = copies.shape[0]
    span_count = copies.shape[1]
    head_count = memory.shape[3]
    flat_rows = copies.reshape(-1, E).astype(jnp.float32)
    normed = rms_rows(flat_rows).astype(jnp.bfloat16)
    enc_query = jnp.dot(normed, query_w, preferred_element_type=jnp.float32).astype(jnp.bfloat16)
    enc_query = enc_query.reshape(groups, span_count, PT, head_count, EHD)
    scores = jnp.einsum(
        "gcqhd,ckhd->gchqk", enc_query, memory[:, :, 0], preferred_element_type=jnp.float32
    ) / math.sqrt(EHD)
    weights = softmax_rows(scores).astype(jnp.bfloat16)
    mixed_heads = jnp.einsum(
        "gchqk,ckhd->gcqhd", weights, memory[:, :, 1], preferred_element_type=jnp.float32
    )
    mixed_heads = mixed_heads.astype(jnp.bfloat16).reshape(-1, head_count * EHD)
    branch = lax.dot_general(
        mixed_heads, out_w, (((1,), (1,)), ((), ())), preferred_element_type=jnp.float32
    )
    return (flat_rows, branch)


def body(
    span_states,
    span_queries,
    span_memory,
    passages,
    neighbours,
    enc_query_w,
    enc_out_w,
    kv_weight,
    out_weight,
):
    device_count = lax.axis_size("span")
    head_index = lax.axis_index("head")
    span_count = neighbours.shape[0]
    owners = neighbours // PS_DEV
    local_ids = neighbours % PS_DEV
    wanted = wanted_slots(owners.reshape(-1), local_ids.reshape(-1), device_count)[:, None]
    fetched = fetch_passages(wanted, passages)
    own_owner = lax.dynamic_index_in_dim(owners, head_index, 1, keepdims=False)
    copies = fetched[own_owner, 0][None]
    query_full, out_full = (
        lax.all_gather(enc_query_w, "head", axis=1, tiled=True),
        lax.all_gather(enc_out_w, "head", axis=1, tiled=True),
    )
    memory_full = lax.all_gather(span_memory, "head", axis=2, tiled=True)
    memory = memory_full.reshape(span_count, CT, 2, -1, EHD)
    own_rows, own_branch = encode_branch(copies, memory, query_full, out_full)
    encoded = rms_rows(own_rows + own_branch).astype(jnp.bfloat16)
    all_encoded = lax.all_gather(encoded[None], "head", axis=0, tiled=True)
    flat_encoded = all_encoded.reshape(-1, E)
    dec_kv = jnp.einsum(
        "re,esc->rsc",
        flat_encoded,
        lax.all_gather(kv_weight, "span", axis=2, tiled=True),
        preferred_element_type=jnp.float32,
    ).astype(jnp.bfloat16)
    head_count = span_queries.shape[1] // HD
    dec_kv = dec_kv.reshape(NB, span_count, PT, 2, head_count, HD)
    dec_query = span_queries.reshape(span_count, CT, head_count, HD)
    scores = jnp.einsum(
        "cqhd,ncphd->chqnp", dec_query, dec_kv[:, :, :, 0], preferred_element_type=jnp.float32
    ) / math.sqrt(HD)
    scores = scores.reshape(span_count, head_count, CT, NB * PT)
    weights = softmax_rows(scores).astype(jnp.bfloat16).reshape(span_count, head_count, CT, NB, PT)
    attended = jnp.einsum(
        "chqnp,ncphd->cqhd", weights, dec_kv[:, :, :, 1], preferred_element_type=jnp.float32
    )
    attended = attended.astype(jnp.bfloat16).reshape(span_count * CT, head_count * HD)
    partial_value = jnp.dot(
        attended,
        lax.all_gather(out_weight, "span", axis=1, tiled=True),
        preferred_element_type=jnp.float32,
    )
    summed = lax.psum_scatter(
        partial_value.astype(jnp.bfloat16), "head", scatter_dimension=1, tiled=True
    ).astype(jnp.float32)
    return (span_states.astype(jnp.float32) + summed).astype(jnp.bfloat16)


def solution(mesh):
    placed = (
        P(("groups", "span"), "head"),
        P(("groups", "span"), "head"),
        P(("groups", "span"), None, "head"),
        P(("groups", "span"), None),
        P(("groups", "span"), None),
        P(None, "head"),
        P(None, "head"),
        P(None, None, ("head", "span")),
        P("head", "span"),
    )
    return jax.shard_map(
        body, mesh=mesh, in_specs=placed, out_specs=P(("groups", "span"), "head"), check_vma=False
    )
```

profile of v0, /device:TPU:0, one launch (start us, length us, event | category | flops | bytes accessed | tf_op | source)
XLA Modules:
  0.0 270.7 jit_solution(14112811568693671814)
XLA Ops:
  6.5 0.7 all-gather.6.cloned.1.call-update
  7.3 0.7 all-gather.8.cloned.1.call-update
  8.1 0.8 copy.54
  9.9 13.6 %all_to_all.14 = s32[8,1,1]{2,1,0:T(1,128)S(1)} all-to-all(s32[8,1,1]{2,1,0:T(1,128)S(1)} %copy.48), channel_id=1, replica_groups=mesh['groups'=2,'span'=8,'head'=2] {'span'}, dimensions={0} | all-to-all | bytes 64 | tf_op jit(solution)/shard_map/all_to_all | solution.py:34
  23.7 2.0 gather_fusion
  25.7 4.4 %all-to-all-start.1 = ((bf16[8,1,128,896]{3,2,1,0:T(8,128)(2,1)}), bf16[8,1,128,896]{3,2,1,0:T(8,128)(2,1)}, u32[]{:S(2)}, u32[]{:S(2)}) async-start(bf16[8,1,128,896]{3,2,1,0:T(8,128)(2,1)} %bitcast.92), calls=%async_computation.1 | async-start | bytes 3670016 | tf_op jit(solution)/shard_map/all_to_all | solution.py:35
  30.2 2.1 all_gather.19
  32.8 1.7 fusion.25
  34.4 1.1 copy.66
  35.8 0.7 bitcast_bitcast_fusion
  36.5 49.9 %all-to-all-done.1 = bf16[8,1,128,896]{3,2,1,0:T(8,128)(2,1)} async-done(((bf16[8,1,128,896]{3,2,1,0:T(8,128)(2,1)}), bf16[8,1,128,896]{3,2,1,0:T(8,128)(2,1)}, u32[]{:S(2)}, u32[]{:S(2)}) %all-to-all-start.1) | async-done | bytes 1835040 | tf_op jit(solution)/shard_map/all_to_all | solution.py:35
  86.4 2.1 gather_fusion.1
  88.9 3.0 %convolution_convert_fusion.3 = bf16[256,896]{1,0:T(8,128)(2,1)} fusion(bf16[256,896]{1,0:T(8,128)(2,1)S(1)} %fusion.8, bf16[896,896]{0,1:T(8,128)(2,1)} %all-gather.6.cloned.1.call-done), kind=kOutput, calls=%fused_computation.10 | convolution fusion | flops 411271168 | bytes 2523136 | tf_op jit(solution)/shard_map/dot_general | solution.py:44
  91.9 1.8 reshape.118
  93.7 1.8 fusion.26
  96.5 2.2 multiply_reduce_fusion
  98.9 2.5 all-gather
  101.4 23.2 %all-gather.10.cloned.1.call-done = bf16[896,2,1024]{2,0,1:T(8,128)(2,1)} async-done(((bf16[896,2,128]{2,0,1:T(8,128)(2,1)}), bf16[896,2,1024]{2,0,1:T(8,128)(2,1)}) %all-gather.10.cloned.1.call-update) | async-done | bytes 3670032 | tf_op jit(solution)/shard_map/all_gather | solution.py:93
  124.5 4.4 %convolution_convert_fusion.1 = bf16[512,2,1024]{2,0,1:T(8,128)(2,1)S(1)} fusion(bf16[896,2,1024]{2,0,1:T(8,128)(2,1)} %all-gather.10.cloned.1.call-done, bf16[512,896]{1,0:T(8,128)(2,1)S(1)} %all-gather), kind=kOutput, calls=%fused_computation.3 | convolution fusion | flops 1880096768 | bytes 6684672 | tf_op jit(solution)/shard_map/re,esc->rsc/dot_general | solution.py:90
  129.7 0.8 copy-done.1
  132.1 117.6 %all-gather.12.cloned.1.call-done = bf16[1024,4096]{1,0:T(8,128)(2,1)} async-done(((bf16[1024,512]{1,0:T(8,128)(2,1)}), bf16[1024,4096]{1,0:T(8,128)(2,1)}) %all-gather.12.cloned.1.call-update) | async-done | bytes 8388624 | tf_op jit(solution)/shard_map/all_gather | solution.py:110
  249.7 5.8 %convolution_convert_fusion = bf16[128,4096]{1,0:T(8,128)(2,1)} fusion(bf16[1024,4096]{1,0:T(8,128)(2,1)} %all-gather.12.cloned.1.call-done, bf16[16,8,8,128]{3,2,1,0:T(8,128)(2,1)S(1)} %bitcast.95), kind=kOutput, calls=%fused_computation.2 | convolution fusion | flops 1074266112 | bytes 9699328 | tf_op jit(solution)/shard_map/dot_general | solution.py:108
  255.5 6.7 %reduce-scatter.2.cloned.1.call-done = bf16[128,2048]{1,0:T(8,128)(2,1)} async-done(((bf16[128,4096]{1,0:T(8,128)(2,1)}), bf16[128,2048]{1,0:T(8,128)(2,1)}) %reduce-scatter.2.cloned.1.call-update) | async-done | bytes 524304 | tf_op jit(solution)/shard_map/reduce_scatter | solution.py:113
  262.2 2.0 add_convert_fusion
  (49 shorter events, 5.8 us)
Async XLA Ops:
  6.5 17.2 %copy-start = (bf16[1024,896]{1,0:T(8,128)(2,1)S(1)}, bf16[1024,896]{1,0:T(8,128)(2,1)}, u32[]{:S(2)}) copy-start(bf16[1024,896]{1,0:T(8,128)(2,1)} %param.12) | copy-start | bytes 5505028
  6.5 1.5 copy-start.4
  6.5 3.0 %copy-start.7 = (s32[2,2]{1,0:T(2,128)S(1)}, s32[2,2]{1,0:T(2,128)}, u32[]{:S(2)}) copy-start(s32[2,2]{1,0:T(2,128)} %param.13) | copy-start | bytes 52
  6.5 82.3 %all-gather.6.cloned.1.call-start = ((), (), s32[]{:S(2)}) async-start(), calls=%async_computation.3 | async-start | bytes 2408448 | tf_op jit(solution)/shard_map/all_gather | solution.py:81
  7.3 89.2 %all-gather.8.cloned.1.call-start = ((), (), s32[]{:S(2)}) async-start(), calls=%async_computation.4 | async-start | bytes 2408448 | tf_op jit(solution)/shard_map/all_gather | solution.py:82
  8.0 116.5 %all-gather.10.cloned.1.call-start = ((), (), s32[]{:S(2)}) async-start(), calls=%async_computation.5 | async-start | bytes 4128768 | tf_op jit(solution)/shard_map/all_gather | solution.py:93
  8.9 240.8 %all-gather.12.cloned.1.call-start = ((), (), s32[]{:S(2)}) async-start(), calls=%async_computation.6 | async-start | bytes 9437184 | tf_op jit(solution)/shard_map/all_gather | solution.py:110
  25.7 4.5 %copy-start.6 = (bf16[128,2,448]{0,2,1:T(8,128)(2,1)S(1)}, bf16[128,2,448]{0,2,1:T(8,128)(2,1)}, u32[]{:S(2)}) copy-start(bf16[128,2,448]{0,2,1:T(8,128)(2,1)} %param.11) | copy-start | bytes 688132
  25.7 60.7 %all-to-all-start.1 = ((bf16[8,1,128,896]{3,2,1,0:T(8,128)(2,1)}), bf16[8,1,128,896]{3,2,1,0:T(8,128)(2,1)}, u32[]{:S(2)}, u32[]{:S(2)}) async-start(bf16[8,1,128,896]{3,2,1,0:T(8,128)(2,1)} %bitcast.92), calls=%async_computation.1 | async-start | bytes 3670016 | tf_op jit(solution)/shard_map/all_to_all | solution.py:35
  30.2 232.1 %reduce-scatter.2.cloned.1.call-start = ((), (), s32[]{:S(2)}) async-start(), calls=%async_computation.7 | async-start | bytes 1572864 | tf_op jit(solution)/shard_map/reduce_scatter | solution.py:113
  32.4 3.2 %copy-start.5 = (bf16[128,1024]{1,0:T(8,128)(2,1)S(1)}, bf16[128,1024]{1,0:T(8,128)(2,1)}, u32[]{:S(2)}) copy-start(bf16[128,1024]{1,0:T(8,128)(2,1)} %param.10) | copy-start | bytes 786436
  93.7 2.0 copy-start.3
  129.5 1.0 copy-start.1
  249.7 12.5 %copy-start.2 = (bf16[128,2048]{1,0:T(8,128)(2,1)S(1)}, bf16[128,2048]{1,0:T(8,128)(2,1)}, u32[]{:S(2)}) copy-start(bf16[128,2048]{1,0:T(8,128)(2,1)} %param.9) | copy-start | bytes 1572868
Sparse Core Ops, SparseCore 0:
  8.9 12.5 all-gather.5
  23.0 11.0 all-gather.7
  36.1 88.3 all-gather.9
  126.4 123.2 all-gather.11
  255.6 6.5 reduce-scatter.1
where the time goes:
time: 271 us
  waiting for transfers between devices  199 us (73%)
  matrix products  18.5 us (7%)
  blocking collectives  18.2 us (7%)
  between operations  13.4 us (5%)
  local copies, waits for them, and re-layouts  13.1 us (5%)
  starting transfers between devices  4.61 us (2%)
  other arithmetic  3.53 us (1%)
    all_gather x1, waiting for transfers between devices, body(): lax.all_gather(out_weight, 'span', axis=1, tiled=True)  118 us
    all_to_all x1, waiting for transfers between devices, fetch_passages(): lax.all_to_all(picked, 'span', split_axis=0, concat_axis=0, tiled=True)  49.9 us
    all_gather x1, waiting for transfers between devices, body(): lax.all_gather(kv_weight, 'span', axis=2, tiled=True)  23.2 us
    all_to_all x1, blocking collectives, fetch_passages(): lax.all_to_all(wanted, 'span', split_axis=0, concat_axis=0, tiled=True)  13.6 us
    reduce_scatter x1, waiting for transfers between devices, body(): lax.psum_scatter(partial_value.astype(jnp.bfloat16), 'head', scatter_dime...  6.73 us
    dot_general x1, matrix products, body(): jnp.dot(attended, lax.all_gather(out_weight, 'span', axis=1, tiled=True),...  5.75 us
  transfers between devices with their start and end apart: 6, of which 4 were waited for; matrix products, arithmetic and copies ran while one was open for 10% of the time, Pallas kernels for 0%

commit v1 on v0

--- a/solution.py
+++ b/solution.py
@@ -12,6 +12,30 @@
 NB = 2
 PS_DEV = 8
 epsilon = 1e-06
+
+
+def put_the_tables(view, mesh_dim):
+    o_now, z_new, extra = (lax.psum(1, axis_name=mesh_dim), lax.axis_index(mesh_dim), view.shape[2])
+    fields = tuple((w * o_now if q == 2 else w for q, w in enumerate(view.shape)))
+    now = lax.dynamic_update_slice_in_dim(
+        jnp.zeros(fields, view.dtype), view, z_new * extra, axis=2
+    )
+    passed = a_next = view
+    dev_i = 1
+    while dev_i < o_now // 2 + 1:
+        passed = lax.ppermute(
+            passed, mesh_dim, perm=tuple(((q, (q + 1) % o_now) for q in range(o_now)))
+        )
+        now = lax.dynamic_update_slice_in_dim(now, passed, (z_new - dev_i) % o_now * extra, axis=2)
+        if 2 * dev_i < o_now:
+            a_next = lax.ppermute(
+                a_next, axis_name=mesh_dim, perm=tuple(((q, (q - 1) % o_now) for q in range(o_now)))
+            )
+            now = lax.dynamic_update_slice_in_dim(
+                now, a_next, (z_new + dev_i) % o_now * extra, axis=2
+            )
+        dev_i += 1
+    return now
 
 
 def rms_rows(values):
@@ -90,7 +114,7 @@
     dec_kv = jnp.einsum(
         "re,esc->rsc",
         flat_encoded,
-        lax.all_gather(kv_weight, "span", axis=2, tiled=True),
+        put_the_tables(kv_weight, "span"),
         preferred_element_type=jnp.float32,
     ).astype(jnp.bfloat16)
     head_count = span_queries.shape[1] // HD

time: 271 us -> 250 us (0.923)
  waiting for transfers between devices: 199 us -> 148 us
  starting transfers between devices: 4.61 us -> 21.3 us
  local copies, waits for them, and re-layouts: 13.1 us -> 24.1 us
    ppermute x0 -> x7, waiting for transfers between devices: none -> 88.9 us  [the longest x4 88.9 us: put_the_tables(): lax.ppermute(passed, mesh_dim, perm=tuple(((q, (q + 1) % o_now) for q in...]
    all_gather x1, waiting for transfers between devices: 118 us -> 48.2 us  [body(): lax.all_gather(out_weight, 'span', axis=1, tiled=True)]
    all_to_all x1, waiting for transfers between devices: 49.9 us -> 0.01 us  [fetch_passages(): lax.all_to_all(picked, 'span', split_axis=0, concat_axis=0, tiled=True)]
    all_gather x1 -> x0, waiting for transfers between devices: 23.2 us -> none  [body(): lax.all_gather(kv_weight, 'span', axis=2, tiled=True)]
    ppermute x0 -> x7, starting transfers between devices: none -> 16.7 us  [the longest x3 12.4 us: put_the_tables(): lax.ppermute(a_next, axis_name=mesh_dim, perm=tuple(((q, (q - 1) % o_now)...]
    dynamic_update_slice x0 -> x8, local copies, waits for them, and re-layouts: none -> 10.2 us  [the longest x4 4.56 us: put_the_tables(): lax.dynamic_update_slice_in_dim(now, passed, (z_new - dev_i) % o_now * ex...]
  transfers between devices with their start and end apart: 6 -> 12, of which waited for: 4 -> 6; matrix products, arithmetic and copies ran while one was open for 10% -> 16% of each run, Pallas kernels for 0% -> 0%
where the time goes in v1:
time: 250 us; the launch traced here: 249 us
  waiting for transfers between devices  148 us (59%)
  local copies, waits for them, and re-layouts  24.1 us (10%)
  starting transfers between devices  21.3 us (9%)
  matrix products  19.5 us (8%)
  blocking collectives  18.4 us (7%)
  between operations  13.4 us (5%)
  other arithmetic  4.21 us (2%)
    ppermute x4, waiting for transfers between devices, put_the_tables(): lax.ppermute(passed, mesh_dim, perm=tuple(((q, (q + 1) % o_now) for q in...  88.9 us
    all_gather x1, waiting for transfers between devices, body(): lax.all_gather(out_weight, 'span', axis=1, tiled=True)  48.2 us
    all_to_all x1, blocking collectives, fetch_passages(): lax.all_to_all(wanted, 'span', split_axis=0, concat_axis=0, tiled=True)  13.6 us
    ppermute x3, starting transfers between devices, put_the_tables(): lax.ppermute(a_next, axis_name=mesh_dim, perm=tuple(((q, (q - 1) % o_now)...  12.4 us
    reduce_scatter x1, waiting for transfers between devices, body(): lax.psum_scatter(partial_value.astype(jnp.bfloat16), 'head', scatter_dime...  9.03 us
    dot_general x1, matrix products, body(): jnp.dot(attended, lax.all_gather(out_weight, 'span', axis=1, tiled=True),...  5.76 us
  transfers between devices with their start and end apart: 12, of which 6 were waited for; matrix products, arithmetic and copies ran while one was open for 16% of the time, Pallas kernels for 0%

profile of v1, /device:TPU:0, one launch (start us, length us, event | category | flops | bytes accessed | tf_op | source)
XLA Modules:
  0.0 249.2 jit_solution(11201915900183707508)
XLA Ops:
  9.8 13.6 %all_to_all.14 = s32[8,1,1]{2,1,0:T(1,128)S(1)} all-to-all(s32[8,1,1]{2,1,0:T(1,128)S(1)} %copy.76), channel_id=1, replica_groups=mesh['groups'=2,'span'=8,'head'=2] {'span'}, dimensions={0} | all-to-all | bytes 64 | tf_op jit(solution)/shard_map/all_to_all | solution.py:58
  23.6 2.0 gather_fusion
  25.6 4.5 %all-to-all-start.1 = ((bf16[8,1,128,896]{3,2,1,0:T(8,128)(2,1)}), bf16[8,1,128,896]{3,2,1,0:T(8,128)(2,1)}, u32[]{:S(2)}, u32[]{:S(2)}) async-start(bf16[8,1,128,896]{3,2,1,0:T(8,128)(2,1)} %bitcast.92), calls=%async_computation.1 | async-start | bytes 3670016 | tf_op jit(solution)/shard_map/all_to_all | solution.py:59
  32.0 2.9 %collective-permute-start.1 = (bf16[896,2,128]{2,1,0:T(2,128)(2,1)}, bf16[896,2,128]{2,1,0:T(2,128)(2,1)}, u32[]{:S(2)}, u32[]{:S(2)}) collective-permute-start(bf16[896,2,128]{2,1,0:T(2,128)(2,1)} %param.16), channel_id=1, source_target_pairs={{0,14},{2,0},{4,2},{6,4},{8,6},{10,8},{12,10},{14,12},{1,15},{3,1}... | collective-permute-start | bytes 1376264 | tf_op jit(solution)/shard_map/ppermute | solution.py:31
  34.9 2.1 all_gather.16
  41.2 2.3 broadcast_in_dim.34
  43.5 1.9 copy_dynamic-update-slice_fusion.7
  45.5 50.8 %collective-permute-done = bf16[896,2,128]{2,1,0:T(2,128)(2,1)} collective-permute-done((bf16[896,2,128]{2,1,0:T(2,128)(2,1)}, bf16[896,2,128]{2,1,0:T(2,128)(2,1)}, u32[]{:S(2)}, u32[]{:S(2)}) %collective-permute-start) | collective-permute-done | bytes 458784 | tf_op jit(solution)/shard_map/ppermute | solution.py:26
  96.2 4.7 %collective-permute-start.3 = (bf16[896,2,128]{2,1,0:T(2,128)(2,1)}, bf16[896,2,128]{2,1,0:T(2,128)(2,1)S(1)}, u32[]{:S(2)}, u32[]{:S(2)}) collective-permute-start(bf16[896,2,128]{2,1,0:T(2,128)(2,1)} %collective-permute-done.1), channel_id=1, source_target_pairs={{0,14},{2,0},{4,2},{6,4},{8,6},{10,8},{12,10},{14,12},{1,15},{3,1}... | collective-permute-start | bytes 1376264 | tf_op jit(solution)/shard_map/ppermute | solution.py:31
  100.9 1.9 copy_dynamic-update-slice_fusion.6
  104.8 15.4 %collective-permute-done.2 = bf16[896,2,128]{2,1,0:T(2,128)(2,1)S(1)} collective-permute-done((bf16[896,2,128]{2,1,0:T(2,128)(2,1)}, bf16[896,2,128]{2,1,0:T(2,128)(2,1)S(1)}, u32[]{:S(2)}, u32[]{:S(2)}) %collective-permute-start.2) | collective-permute-done | bytes 458784 | tf_op jit(solution)/shard_map/ppermute | solution.py:26
  120.2 4.7 %collective-permute-start.5 = (bf16[896,2,128]{2,1,0:T(2,128)(2,1)S(1)}, bf16[896,2,128]{2,1,0:T(2,128)(2,1)S(1)}, u32[]{:S(2)}, u32[]{:S(2)}) collective-permute-start(bf16[896,2,128]{2,1,0:T(2,128)(2,1)S(1)} %collective-permute-done.3), channel_id=1, source_target_pairs={{0,14},{2,0},{4,2},{6,4},{8,6},{10,8},{12,10},{14,12},{1,15},{3,1}... | collective-permute-start | bytes 1376264 | tf_op jit(solution)/shard_map/ppermute | solution.py:31
  126.7 11.5 %collective-permute-done.4 = bf16[896,2,128]{2,1,0:T(2,128)(2,1)S(1)} collective-permute-done((bf16[896,2,128]{2,1,0:T(2,128)(2,1)S(1)}, bf16[896,2,128]{2,1,0:T(2,128)(2,1)S(1)}, u32[]{:S(2)}, u32[]{:S(2)}) %collective-permute-start.4) | collective-permute-done | bytes 458784 | tf_op jit(solution)/shard_map/ppermute | solution.py:26
  138.2 2.5 collective-permute-start.6
  142.4 11.2 %collective-permute-done.6 = bf16[896,2,128]{2,1,0:T(2,128)(2,1)S(1)} collective-permute-done((bf16[896,2,128]{2,1,0:T(2,128)(2,1)S(1)}, bf16[896,2,128]{2,1,0:T(2,128)(2,1)S(1)}, u32[]{:S(2)}, u32[]{:S(2)}) %collective-permute-start.6) | collective-permute-done | bytes 458784 | tf_op jit(solution)/shard_map/ppermute | solution.py:26
  154.6 2.1 gather_fusion.1
  157.1 2.9 %convolution_convert_fusion.3 = bf16[256,896]{1,0:T(8,128)(2,1)} fusion(bf16[256,896]{1,0:T(8,128)(2,1)S(1)} %fusion.8, bf16[896,896]{0,1:T(8,128)(2,1)} %all-gather.5.cloned.1.call-done), kind=kOutput, calls=%fused_computation.10 | convolution fusion | flops 411271168 | bytes 2523136 | tf_op jit(solution)/shard_map/dot_general | solution.py:68
  165.6 2.2 multiply_reduce_fusion
  168.0 2.6 %all-gather = bf16[512,896]{1,0:T(8,128)(2,1)S(1)} all-gather(bf16[256,896]{1,0:T(8,128)(2,1)S(1)} %multiply_convert_fusion), channel_id=2, replica_groups=mesh['groups'=2,'span'=8,'head'=2] {'head'}, dimensions={0}, use_global_device_ids=true | all-gather | bytes 1376256 | tf_op jit(solution)/shard_map/all_gather | solution.py:112
  170.6 4.4 %convolution_convert_fusion.1 = bf16[512,2,1024]{2,0,1:T(8,128)(2,1)S(1)} fusion(bf16[896,2,1024]{2,0,1:T(8,128)(2,1)} %copy_dynamic-update-slice_fusion, bf16[512,896]{1,0:T(8,128)(2,1)S(1)} %all-gather), kind=kOutput, calls=%fused_computation.3 | convolution fusion | flops 1880096768 | bytes 6684672 | tf_op jit(solution)/shard_map/re,esc->rsc/dot_general | solution.py:114
  177.7 48.2 %all-gather.9.cloned.1.call-done = bf16[1024,4096]{1,0:T(8,128)(2,1)} async-done(((bf16[1024,512]{1,0:T(8,128)(2,1)}), bf16[1024,4096]{1,0:T(8,128)(2,1)}) %all-gather.9.cloned.1.call-update) | async-done | bytes 8388624 | tf_op jit(solution)/shard_map/all_gather | solution.py:134
  225.9 5.8 %convolution_convert_fusion = bf16[128,4096]{1,0:T(8,128)(2,1)} fusion(bf16[1024,4096]{1,0:T(8,128)(2,1)} %all-gather.9.cloned.1.call-done, bf16[16,8,8,128]{3,2,1,0:T(8,128)(2,1)S(1)} %bitcast.95), kind=kOutput, calls=%fused_computation.2 | convolution fusion | flops 1074266112 | bytes 9699328 | tf_op jit(solution)/shard_map/dot_general | solution.py:132
  231.7 9.0 %reduce-scatter.2.cloned.1.call-done = bf16[128,2048]{1,0:T(8,128)(2,1)} async-done(((bf16[128,4096]{1,0:T(8,128)(2,1)}), bf16[128,2048]{1,0:T(8,128)(2,1)}) %reduce-scatter.2.cloned.1.call-update) | async-done | bytes 524304 | tf_op jit(solution)/shard_map/reduce_scatter | solution.py:137
  240.7 2.0 add_convert_fusion
  (62 shorter events, 24.3 us)
Async XLA Ops:
  6.5 17.1 %copy-start = (bf16[1024,896]{1,0:T(8,128)(2,1)S(1)}, bf16[1024,896]{1,0:T(8,128)(2,1)}, u32[]{:S(2)}) copy-start(bf16[1024,896]{1,0:T(8,128)(2,1)} %param.12) | copy-start | bytes 5505028
  6.5 150.5 %all-gather.5.cloned.1.call-start = ((), (), s32[]{:S(2)}) async-start(), calls=%async_computation.3 | async-start | bytes 2408448 | tf_op jit(solution)/shard_map/all_gather | solution.py:105
  7.3 158.3 %all-gather.7.cloned.1.call-start = ((), (), s32[]{:S(2)}) async-start(), calls=%async_computation.4 | async-start | bytes 2408448 | tf_op jit(solution)/shard_map/all_gather | solution.py:106
  8.0 217.9 %all-gather.9.cloned.1.call-start = ((), (), s32[]{:S(2)}) async-start(), calls=%async_computation.5 | async-start | bytes 9437184 | tf_op jit(solution)/shard_map/all_gather | solution.py:134
  23.6 11.3 %copy-start.4 = (bf16[128,2,448]{0,2,1:T(8,128)(2,1)S(1)}, bf16[128,2,448]{0,2,1:T(8,128)(2,1)}, u32[]{:S(2)}) copy-start(bf16[128,2,448]{0,2,1:T(8,128)(2,1)} %param.11) | copy-start | bytes 688132
  25.6 14.6 %copy-start.3 = (bf16[128,1024]{1,0:T(8,128)(2,1)S(1)}, bf16[128,1024]{1,0:T(8,128)(2,1)}, u32[]{:S(2)}) copy-start(bf16[128,1024]{1,0:T(8,128)(2,1)} %param.10) | copy-start | bytes 786436
  25.6 128.9 %all-to-all-start.1 = ((bf16[8,1,128,896]{3,2,1,0:T(8,128)(2,1)}), bf16[8,1,128,896]{3,2,1,0:T(8,128)(2,1)}, u32[]{:S(2)}, u32[]{:S(2)}) async-start(bf16[8,1,128,896]{3,2,1,0:T(8,128)(2,1)} %bitcast.92), calls=%async_computation.1 | async-start | bytes 3670016 | tf_op jit(solution)/shard_map/all_to_all | solution.py:59
  30.1 210.6 %reduce-scatter.2.cloned.1.call-start = ((), (), s32[]{:S(2)}) async-start(), calls=%async_computation.6 | async-start | bytes 1572864 | tf_op jit(solution)/shard_map/reduce_scatter | solution.py:137
  30.1 66.1 %collective-permute-start = (bf16[896,2,128]{2,1,0:T(2,128)(2,1)}, bf16[896,2,128]{2,1,0:T(2,128)(2,1)}, u32[]{:S(2)}, u32[]{:S(2)}) collective-permute-start(bf16[896,2,128]{2,1,0:T(2,128)(2,1)} %param.16), channel_id=1, source_target_pairs={{0,2},{2,4},{4,6},{6,8},{8,10},{10,12},{12,14},{14,0},{1,3},{3,5},... | collective-permute-start | bytes 1376264 | tf_op jit(solution)/shard_map/ppermute | solution.py:26
  32.0 64.2 %collective-permute-start.1 = (bf16[896,2,128]{2,1,0:T(2,128)(2,1)}, bf16[896,2,128]{2,1,0:T(2,128)(2,1)}, u32[]{:S(2)}, u32[]{:S(2)}) collective-permute-start(bf16[896,2,128]{2,1,0:T(2,128)(2,1)} %param.16), channel_id=1, source_target_pairs={{0,14},{2,0},{4,2},{6,4},{8,6},{10,8},{12,10},{14,12},{1,15},{3,1}... | collective-permute-start | bytes 1376264 | tf_op jit(solution)/shard_map/ppermute | solution.py:31
  96.2 24.0 %collective-permute-start.2 = (bf16[896,2,128]{2,1,0:T(2,128)(2,1)}, bf16[896,2,128]{2,1,0:T(2,128)(2,1)S(1)}, u32[]{:S(2)}, u32[]{:S(2)}) collective-permute-start(bf16[896,2,128]{2,1,0:T(2,128)(2,1)} %collective-permute-done), channel_id=1, source_target_pairs={{0,2},{2,4},{4,6},{6,8},{8,10},{10,12},{12,14},{14,0},{1,3},{3,5},... | collective-permute-start | bytes 1376264 | tf_op jit(solution)/shard_map/ppermute | solution.py:26
  96.2 24.0 %collective-permute-start.3 = (bf16[896,2,128]{2,1,0:T(2,128)(2,1)}, bf16[896,2,128]{2,1,0:T(2,128)(2,1)S(1)}, u32[]{:S(2)}, u32[]{:S(2)}) collective-permute-start(bf16[896,2,128]{2,1,0:T(2,128)(2,1)} %collective-permute-done.1), channel_id=1, source_target_pairs={{0,14},{2,0},{4,2},{6,4},{8,6},{10,8},{12,10},{14,12},{1,15},{3,1}... | collective-permute-start | bytes 1376264 | tf_op jit(solution)/shard_map/ppermute | solution.py:31
  120.2 18.0 %collective-permute-start.4 = (bf16[896,2,128]{2,1,0:T(2,128)(2,1)S(1)}, bf16[896,2,128]{2,1,0:T(2,128)(2,1)S(1)}, u32[]{:S(2)}, u32[]{:S(2)}) collective-permute-start(bf16[896,2,128]{2,1,0:T(2,128)(2,1)S(1)} %collective-permute-done.2), channel_id=1, source_target_pairs={{0,2},{2,4},{4,6},{6,8},{8,10},{10,12},{12,14},{14,0},{1,3},{3,5},... | collective-permute-start | bytes 1376264 | tf_op jit(solution)/shard_map/ppermute | solution.py:26
  120.2 21.3 %collective-permute-start.5 = (bf16[896,2,128]{2,1,0:T(2,128)(2,1)S(1)}, bf16[896,2,128]{2,1,0:T(2,128)(2,1)S(1)}, u32[]{:S(2)}, u32[]{:S(2)}) collective-permute-start(bf16[896,2,128]{2,1,0:T(2,128)(2,1)S(1)} %collective-permute-done.3), channel_id=1, source_target_pairs={{0,14},{2,0},{4,2},{6,4},{8,6},{10,8},{12,10},{14,12},{1,15},{3,1}... | collective-permute-start | bytes 1376264 | tf_op jit(solution)/shard_map/ppermute | solution.py:31
  138.2 15.5 %collective-permute-start.6 = (bf16[896,2,128]{2,1,0:T(2,128)(2,1)S(1)}, bf16[896,2,128]{2,1,0:T(2,128)(2,1)S(1)}, u32[]{:S(2)}, u32[]{:S(2)}) collective-permute-start(bf16[896,2,128]{2,1,0:T(2,128)(2,1)S(1)} %collective-permute-done.4), channel_id=1, source_target_pairs={{0,2},{2,4},{4,6},{6,8},{8,10},{10,12},{12,14},{14,0},{1,3},{3,5},... | collective-permute-start | bytes 1376264 | tf_op jit(solution)/shard_map/ppermute | solution.py:26
  175.1 1.0 copy-start.1
  225.9 14.8 %copy-start.2 = (bf16[128,2048]{1,0:T(8,128)(2,1)S(1)}, bf16[128,2048]{1,0:T(8,128)(2,1)}, u32[]{:S(2)}) copy-start(bf16[128,2048]{1,0:T(8,128)(2,1)} %param.9) | copy-start | bytes 1572868
Sparse Core Ops, SparseCore 0:
  8.9 12.5 all-gather.4
  23.0 11.0 all-gather.6
  36.1 189.7 all-gather.8
  231.8 8.8 reduce-scatter.1
